TPU v7x, 128 devices: a whole 4x4x4 slice. The times are simulated.
128 devices in a mesh: slot: 16 (over y, z), head: 2 (over x_lo), conv: 4 (over x_hi, core).
Axes of the slice: x: 4 (x_hi: 2, x_lo: 2; x = x_hi * 2 + x_lo), y: 4, z: 4, core: 2. Of those that a mesh axis runs over, the one named last changes fastest.
Arguments:
- queries: bfloat16 [1024, 64, 128], P(('conv', 'slot'), 'head'), may hold values from -96 to 96
- out_grad: bfloat16 [1024, 64, 128], P(('conv', 'slot'), 'head'), may hold values from -768 to 768
- row_positions: int32 [1024], P('conv'), may hold values from 0 to 8191
- slot_offsets: int32 [16384], P('slot'), may hold values from 0 to 16382, as said below
- cache: float32 [2, 16384, 4, 128], P(None, 'slot', 'head'), may hold values from -12 to 12
- first_moment: float32 [2, 16384, 4, 128], P(None, 'slot', 'head'), may hold values from -6 to 6
- second_moment: float32 [2, 16384, 4, 128], P(None, 'slot', 'head'), may hold values from 0.01 to 1000
Outputs:
- new_cache: float32 [2, 16384, 4, 128], P(None, 'slot', 'head')
- new_first_moment: float32 [2, 16384, 4, 128], P(None, 'slot', 'head')
- new_second_moment: float32 [2, 16384, 4, 128], P(None, 'slot', 'head')
- query_grad: float32 [1024, 64, 128], P(('conv', 'slot'), 'head')
Inputs may be any that keep to these rules, and one draw needn't show every extreme that they name: `slot_offsets`: never falls from one slot to the next; its first two entries are 0.
All inputs are finite; a program needn't handle non-finite values.
Results may differ from a plain program's by a relative error of at most 0.012.
The roundings to bfloat16 on the way count: a program that leaves them out, or rounds other values in their place, can miss the bound.
Values may be sent and summed in bfloat16 or wider, within the bound.
A program may use at most 128 MiB of HBM per device.

v0:
```python
import math
import jax
import jax.numpy as jnp
from jax import lax
from jax.sharding import PartitionSpec as P

STEP = 20
learn_rate = 0.01
beta_one = 0.9
beta_two = 0.95
adam_eps = 1e-08
masked_score = -1e30


def merged(x, axis, combine):
    everything = jax.tree.map(lambda part: lax.all_gather(part, axis), x)
    leading = jax.tree.map(lambda part: part[0], everything)

    def lap(k, so_far):
        return combine(so_far, jax.tree.map(lambda part: part[k], everything))

    return lax.fori_loop(1, lax.axis_size(axis), lap, leading)


def merge_pairs(earlier, later):
    largest = jnp.maximum(earlier[0], later[0])
    return (
        largest,
        earlier[1] * jnp.exp(earlier[0] - largest) + later[1] * jnp.exp(later[0] - largest),
    )


def local(queries, out_grad, row_positions, slot_offsets, cache, first_moment, second_moment):
    query_all, grad_all = (
        lax.all_gather(queries, "slot", axis=0, tiled=True),
        lax.all_gather(out_grad, "slot", axis=0, tiled=True),
    )
    total_rows, head_count, head_width = query_all.shape
    kv_count = cache.shape[2]
    group_heads = head_count // kv_count
    score_scale = 1.0 / math.sqrt(head_width)
    block_rows = min(64, total_rows)
    block_count = total_rows // block_rows
    key_half = cache[0].astype(jnp.bfloat16)
    value_half = cache[1].astype(jnp.bfloat16)
    query_blocks = query_all.reshape(block_count, block_rows, kv_count, group_heads, head_width)
    grad_blocks = grad_all.reshape(block_count, block_rows, kv_count, group_heads, head_width)
    visible_all = (slot_offsets[None, :] <= row_positions[:, None]).reshape(
        block_count, block_rows, -1
    )

    def masked_scores(query_block, visible):
        raw_score = (
            jnp.einsum("rkgd,skd->rkgs", query_block, key_half, preferred_element_type=jnp.float32)
            * score_scale
        )
        return jnp.where(visible[:, None, None, :], raw_score, masked_score)

    def weights_from(scores, visible, offset):
        return jnp.where(visible[:, None, None, :], jnp.exp(scores - offset[..., None]), 0.0)

    def gradient_products(grad_block):
        return jnp.einsum(
            "rkgd,skd->rkgs", grad_block, value_half, preferred_element_type=jnp.float32
        )

    def max_pass(inputs):
        query_block, visible = inputs
        scores = masked_scores(query_block, visible)
        largest = jnp.max(scores, axis=-1)
        return (largest, jnp.sum(weights_from(scores, visible, largest), axis=-1))

    largest, denominator = lax.map(max_pass, (query_blocks, visible_all))
    largest, denominator = merged((largest, denominator), "slot", merge_pairs)
    log_total = largest + jnp.log(denominator)

    def product_pass(inputs):
        query_block, grad_block, visible, block_total = inputs
        probability = weights_from(masked_scores(query_block, visible), visible, block_total)
        return jnp.sum(probability * gradient_products(grad_block), axis=-1)

    partial_sum = lax.map(product_pass, (query_blocks, grad_blocks, visible_all, log_total))
    row_sum = lax.psum(partial_sum, "slot")

    def last_pass(running, inputs):
        key_grad, value_grad = running
        query_block, grad_block, visible, block_total, block_sum = inputs
        probability = weights_from(masked_scores(query_block, visible), visible, block_total)
        prob_grad = gradient_products(grad_block)
        score_grad = (probability * (prob_grad - block_sum[..., None])).astype(jnp.bfloat16)
        prob_half = probability.astype(jnp.bfloat16)
        value_grad = value_grad + jnp.einsum(
            "rkgs,rkgd->skd", prob_half, grad_block, preferred_element_type=jnp.float32
        )
        key_grad = (
            key_grad
            + jnp.einsum(
                "rkgs,rkgd->skd", score_grad, query_block, preferred_element_type=jnp.float32
            )
            * score_scale
        )
        query_part = (
            jnp.einsum("rkgs,skd->rkgd", score_grad, key_half, preferred_element_type=jnp.float32)
            * score_scale
        )
        return ((key_grad, value_grad), query_part)

    empty_grad = jnp.zeros(key_half.shape, jnp.float32)
    (key_grad, value_grad), query_parts = lax.scan(
        last_pass,
        (empty_grad, empty_grad),
        (query_blocks, grad_blocks, visible_all, log_total, row_sum),
    )
    query_terms = query_parts.reshape(total_rows, head_count, head_width)
    summed = lax.psum(query_terms, "slot")
    own_rows = queries.shape[0]
    query_grad = lax.dynamic_slice_in_dim(summed, lax.axis_index("slot") * own_rows, own_rows, 0)
    key_total, value_total = lax.psum((key_grad, value_grad), "conv")
    slot_grad = jnp.stack([key_total, value_total])
    new_first = beta_one * first_moment + (1.0 - beta_one) * slot_grad
    new_second = beta_two * second_moment + (1.0 - beta_two) * slot_grad * slot_grad
    first_fix = 1.0 - beta_one**STEP
    second_fix = 1.0 - beta_two**STEP
    new_cache = cache - learn_rate * (new_first / first_fix) / (
        jnp.sqrt(new_second / second_fix) + adam_eps
    )
    return (new_cache, new_first, new_second, query_grad)


def solution(mesh):
    in_specs = (
        P(("conv", "slot"), "head", None),
        P(("conv", "slot"), "head", None),
        P("conv"),
        P("slot"),
        P(None, "slot", "head", None),
        P(None, "slot", "head", None),
        P(None, "slot", "head", None),
    )
    out_specs = (
        P(None, "slot", "head", None),
        P(None, "slot", "head", None),
        P(None, "slot", "head", None),
        P(("conv", "slot"), "head", None),
    )
    return jax.shard_map(local, mesh=mesh, in_specs=in_specs, out_specs=out_specs, check_vma=False)
```

profile of v0, /device:TPU:1, one launch (start us, length us, event | category | flops | bytes accessed | tf_op | source)
XLA Modules:
  0.0 525.3 jit_solution(10511550598650439508)
XLA Ops:
  9.5 1.8 copy.70
  13.1 43.8 %all-gather.5.cloned.1.call-done = bf16[256,32,128]{2,1,0:T(8,128)(2,1)} async-done(((bf16[16,32,128]{2,1,0:T(8,128)(2,1)}), bf16[256,32,128]{2,1,0:T(8,128)(2,1)}) %all-gather.5.cloned.1.call-update) | async-done | bytes 2097168 | tf_op jit(solution)/shard_map/all_gather | solution.py:35
  56.9 3.3 copy.50
  60.1 43.2 %all-gather.7.cloned.1.call-done = bf16[256,32,128]{2,1,0:T(8,128)(2,1)} async-done(((bf16[16,32,128]{2,1,0:T(8,128)(2,1)}), bf16[256,32,128]{2,1,0:T(8,128)(2,1)}) %all-gather.7.cloned.1.call-update) | async-done | bytes 2097168 | tf_op jit(solution)/shard_map/all_gather | solution.py:36
  103.3 3.3 copy.51
  106.6 23.2 %while.54 = (s32[]{:T(128)}, f32[4,64,2,16]{1,3,2,0:T(8,128)S(1)}, f32[4,64,2,16]{1,3,2,0:T(8,128)S(1)}, pred[4,64,1024]{2,1,0:T(8,128)(4,1)S(1)}, bf16[4,64,2,1...) while((s32[]{:T(128)}, f32[4,64,2,16]{1,3,2,0:T(8,128)S(1)}, ...), condition=%wide.region_3.4_spmd, body=%wide.region_0.3_spmd.sunk | while | flops 553644032 | bytes 18210912 | solution.py:73
  106.6 2.8 bitcast_reduce_fusion.2
  109.4 2.8 fusion.87
  112.4 2.8 bitcast_reduce_fusion.2
  115.2 2.8 fusion.87
  118.2 2.8 bitcast_reduce_fusion.2
  121.0 2.8 fusion.87
  124.0 2.8 bitcast_reduce_fusion.2
  126.8 2.8 fusion.87
  129.8 19.1 %all-gather.1 = f32[64,64,2,16]{1,3,2,0:T(8,128)S(1)} all-gather(f32[4,64,2,16]{1,3,2,0:T(8,128)S(1)} %get-tuple-element.272), channel_id=3, replica_groups=mesh['slot'=16,'head'=2,'conv'=4] {'slot'}, dimensions={0}, use_global_device_ids=true | all-gather | bytes 557056 | tf_op jit(solution)/shard_map/all_gather | solution.py:16
  148.9 17.4 %all-gather = f32[64,64,2,16]{1,3,2,0:T(8,128)S(1)} all-gather(f32[4,64,2,16]{1,3,2,0:T(8,128)S(1)} %get-tuple-element.271), channel_id=2, replica_groups=mesh['slot'=16,'head'=2,'conv'=4] {'slot'}, dimensions={0}, use_global_device_ids=true | all-gather | bytes 557056 | tf_op jit(solution)/shard_map/all_gather | solution.py:16
  166.3 1.0 copy-done.4
  167.2 13.9 %while.55 = (s32[]{:T(128)}, f32[4,64,2,16]{1,3,2,0:T(8,128)S(1)}, f32[4,64,2,16]{1,3,2,0:T(8,128)S(1)}, f32[16,4,64,2,16]{2,4,3,1,0:T(8,128)}, f32[16,4,64,2,16...) while((s32[]{:T(128)}, f32[4,64,2,16]{1,3,2,0:T(8,128)S(1)}, f32[4,64,2,16]{1,3,2,0:T(8,128)S(1)}, ...), condition=%wide.region_5.6_spmd, body=%wide.region_4.5_spmd.sunk | while | flops 49157 | bytes 196731 | solution.py:22
  168.1 0.9 fusion.88
  169.1 0.9 fusion.88
  170.0 0.9 fusion.88
  181.5 31.2 %while.56 = (s32[]{:T(128)}, f32[4,64,2,16]{3,1,2,0:T(8,128)}, pred[4,64,1024]{2,1,0:T(8,128)(4,1)S(1)}, bf16[4,64,2,16,128]{4,3,1,2,0:T(8,128)(2,1)}, bf16[1024...) while((s32[]{:T(128)}, f32[4,64,2,16]{3,1,2,0:T(8,128)}, ...), condition=%wide.region_8.9_spmd, body=%wide.region_6.8_spmd.sunk | while | flops 1086322688 | bytes 21397652 | solution.py:82
  181.5 2.4 fusion.93
  183.9 4.7 fusion.94
  189.4 2.4 fusion.93
  191.7 4.7 fusion.94
  197.1 2.4 fusion.93
  199.5 4.7 fusion.94
  204.9 2.4 fusion.93
  207.3 4.7 fusion.94
  212.7 61.1 %psum.28 = f32[4,64,2,16]{3,1,2,0:T(8,128)S(1)} all-reduce(f32[4,64,2,16]{3,1,2,0:T(8,128)} %get-tuple-element.275), channel_id=1, replica_groups=mesh['slot'=16,'head'=2,'conv'=4] {'slot'}, use_global_device_ids=true, to_apply=%region_9.10 | all-reduce | flops 8192 | bytes 65536 | tf_op jit(solution)/shard_map/psum | solution.py:83
  273.8 52.7 %while.57 = (s32[]{:T(128)}, f32[1024,2,128]{0,2,1:T(8,128)S(1)}, f32[1024,2,128]{0,2,1:T(8,128)S(1)}, f32[4,64,2,16,128]{4,3,2,1,0:T(8,128)}, bf16[4,64,2,16,12...) while((s32[]{:T(128)}, f32[1024,2,128]{0,2,1:T(8,128)S(1)}, ...), condition=%wide.region_11.12_spmd.clone, body=%wide.region_10.11_spmd.clone.sunk | while | flops 2711093248 | bytes 59867360 | solution.py:109
  273.9 2.4 fusion.105
  276.4 2.7 fusion.108
  279.1 3.5 fusion.106
  282.5 2.1 fusion.107
  284.7 1.2 fusion.109
  285.9 1.1 copy_dynamic-update-slice_fusion.2
  287.1 2.4 fusion.105
  289.6 2.7 fusion.108
  292.2 3.5 fusion.106
  295.7 2.1 fusion.107
  297.8 1.2 fusion.109
  299.1 1.2 copy_dynamic-update-slice_fusion.2
  300.3 2.4 fusion.105
  302.7 2.7 fusion.108
  305.4 3.5 fusion.106
  308.9 2.1 fusion.107
  311.0 1.2 fusion.109
  312.3 1.1 copy_dynamic-update-slice_fusion.2
  313.4 2.4 fusion.105
  315.9 2.7 fusion.108
  318.6 3.5 fusion.106
  322.1 2.1 fusion.107
  324.2 1.2 fusion.109
  325.4 1.1 copy_dynamic-update-slice_fusion.2
  326.6 1.3 copy.52
  327.9 1.3 copy.53
  329.7 81.8 %all-reduce.6.cloned.1.call-done = (f32[1,1024,2,128]{3,2,1,0:T(2,128)}, f32[1,1024,2,128]{3,2,1,0:T(2,128)}) async-done(((f32[1,1024,2,128]{3,2,1,0:T(2,128)}, f32[1,1024,2,128]{3,2,1,0:T(2,128)}), (f32[1,1024,2,128]{3,2,1,0:T(2,128)}, f32[1,1024,2,128]{3,2,1,0:T(2,128)})) %all-reduce.6.cloned.1.call-update) | async-done | bytes 2097168 | tf_op jit(solution)/shard_map/psum | solution.py:118
  411.5 1.4 constant_dynamic-update-slice_fusion.3
  413.0 1.5 constant_dynamic-update-slice_fusion.2
  414.5 8.0 %divide_subtract_fusion = (f32[2,1024,2,128]{3,2,1,0:T(2,128)}, f32[2,1024,2,128]{3,2,1,0:T(2,128)}, f32[2,1024,2,128]{3,2,1,0:T(2,128)}) fusion(f32[2,1024,2,128]{3,2,1,0:T(2,128)S(1)} %copy-done, f32[2,1024,2,128]{3,2,1,0:T(2,128)S(1)} %constant_dynamic-update-slice_fusion.2, f32[2,1024,2,128]{3,2,1,0:T(2,128)S(1)} %copy-done.1, ...), kind=kLoop, calls=%fused_computation.80 | loop fusion | flops 6291456 | bytes 14680064 | tf_op jit(solution)/shard_map/sub | solution.py:124
  422.5 94.6 %all-reduce.4.cloned.1.call-done = f32[256,32,128]{2,1,0:T(8,128)} async-done(((f32[256,32,128]{2,1,0:T(8,128)}), f32[256,32,128]{2,1,0:T(8,128)}) %all-reduce.4.cloned.1.call-update) | async-done | bytes 4194320 | tf_op jit(solution)/shard_map/psum | solution.py:115
  517.1 1.7 constant_dynamic-slice_fusion
  (103 shorter events, 19.2 us)
Async XLA Ops:
  7.2 49.7 %all-gather.5.cloned.1.call-start = ((), (), s32[]{:S(2)}) async-start(), calls=%async_computation | async-start | bytes 2228224 | tf_op jit(solution)/shard_map/all_gather | solution.py:35
  7.9 95.4 %all-gather.7.cloned.1.call-start = ((), (), s32[]{:S(2)}) async-start(), calls=%async_computation.1 | async-start | bytes 2228224 | tf_op jit(solution)/shard_map/all_gather | solution.py:36
  8.6 402.9 %all-reduce.6.cloned.1.call-start = ((), (), s32[]{:S(2)}) async-start(), calls=%async_computation.3 | async-start | bytes 4194304 | tf_op jit(solution)/shard_map/psum | solution.py:118
  166.2 1.0 copy-start.4
  181.4 92.4 %copy-start.5 = (f32[1024,2,128]{0,2,1:T(8,128)S(1)}, f32[1024,2,128]{0,2,1:T(8,128)}, u32[]{:S(2)}) copy-start(f32[1024,2,128]{0,2,1:T(8,128)} %custom-call.1) | copy-start | bytes 3145732
  181.5 2.4 copy-start.6
  189.3 2.4 copy-start.6
  197.1 2.4 copy-start.6
  204.9 2.4 copy-start.6
  273.9 2.5 copy-start.3
  276.4 2.7 copy-start.7
  287.1 2.5 copy-start.3
  289.5 2.7 copy-start.7
  300.3 2.5 copy-start.3
  302.7 2.7 copy-start.7
  313.4 2.5 copy-start.3
  315.9 2.7 copy-start.7
  329.2 187.9 %all-reduce.4.cloned.1.call-start = ((), (), s32[]{:S(2)}) async-start(), calls=%async_computation.2 | async-start | bytes 8388608 | tf_op jit(solution)/shard_map/psum | solution.py:115
  329.2 85.2 %copy-start = (f32[2,1024,2,128]{3,2,1,0:T(2,128)S(1)}, f32[2,1024,2,128]{3,2,1,0:T(2,128)}, u32[]{:S(2)}) copy-start(f32[2,1024,2,128]{3,2,1,0:T(2,128)} %param.19) | copy-start | bytes 6291460
  411.5 3.0 copy-start.1
  411.5 3.0 copy-start.2
Sparse Core Ops, SparseCore 0:
  10.1 46.6 all-gather.4
  59.0 44.2 all-gather.6
  329.3 82.1 all-reduce.5
  414.7 102.2 all-reduce.3
where the time goes:
time: 527 us; the launch traced here: 525 us
  waiting for transfers between devices  265 us (50%)
  blocking collectives  97.6 us (19%)
  matrix products  87.3 us (17%)
  other arithmetic  33.9 us (6%)
  local copies, waits for them, and re-layouts  26.4 us (5%)
  between operations  13.9 us (3%)
    psum x1, waiting for transfers between devices, local(): summed = lax.psum(query_terms, 'slot')  94.6 us
    psum x1, waiting for transfers between devices, local(): key_total, value_total = lax.psum((key_grad, value_grad), 'conv')  81.8 us
    psum x1, blocking collectives, local(): row_sum = lax.psum(partial_sum, 'slot')  61.1 us
    all_gather x1, waiting for transfers between devices, local(): lax.all_gather(queries, 'slot', axis=0, tiled=True)  43.8 us
    all_gather x1, waiting for transfers between devices, local(): lax.all_gather(out_grad, 'slot', axis=0, tiled=True)  43.2 us
    all_gather x2, blocking collectives, merged(): everything = jax.tree.map(lambda part: lax.all_gather(part, axis), x)  36.5 us
    dot_general x8, matrix products, gradient_products(): jnp.einsum('rkgd,skd->rkgs', grad_block, value_half, preferred_element_ty...  32.8 us
    dot_general x12, matrix products, masked_scores(): jnp.einsum('rkgd,skd->rkgs', query_block, key_half, preferred_element_typ...  30.3 us
  transfers between devices with their start and end apart: 4, of which 4 were waited for; matrix products, arithmetic and copies ran while one was open for 4% of the time, Pallas kernels for 0%

commit v1 on v0

--- a/solution.py
+++ b/solution.py
@@ -10,6 +10,15 @@
 beta_two = 0.95
 adam_eps = 1e-08
 masked_score = -1e30
+_clear_array = lambda page: jnp.concatenate(
+    jax.lax.all_to_all(
+        jnp.stack([page for _ in range(jax.lax.axis_size("slot"))], axis=0),
+        axis_name="slot",
+        split_axis=0,
+        concat_axis=0,
+    ),
+    axis=0,
+)
 
 
 def merged(x, axis, combine):
@@ -32,7 +41,7 @@
 
 def local(queries, out_grad, row_positions, slot_offsets, cache, first_moment, second_moment):
     query_all, grad_all = (
-        lax.all_gather(queries, "slot", axis=0, tiled=True),
+        _clear_array(queries),
         lax.all_gather(out_grad, "slot", axis=0, tiled=True),
     )
     total_rows, head_count, head_width = query_all.shape

time: 527 us -> 476 us (0.903)
  waiting for transfers between devices: 265 us -> 203 us
  starting transfers between devices: 0.16 us -> 8.89 us
    all_gather x1 -> x0, waiting for transfers between devices: 43.8 us -> none  [local(): lax.all_gather(queries, 'slot', axis=0, tiled=True)]
    all_gather x1, waiting for transfers between devices: 43.2 us -> 0.02 us  [local(): lax.all_gather(out_grad, 'slot', axis=0, tiled=True)]
    all_to_all x0 -> x1, waiting for transfers between devices: none -> 25.4 us  [jax.lax.all_to_all(jnp.stack([page for _ in range(jax.lax.axis_size('slot...]
    all_to_all x0 -> x1, starting transfers between devices: none -> 8.77 us  [jax.lax.all_to_all(jnp.stack([page for _ in range(jax.lax.axis_size('slot...]
    unnamed x14 -> x12, local copies, waits for them, and re-layouts: 10.8 us -> 10.6 us
  transfers between devices with their start and end apart: 4 -> 4, of which waited for: 4 -> 3; matrix products, arithmetic and copies ran while one was open for 4% -> 12% of each run, Pallas kernels for 0% -> 0%
where the time goes in v1:
time: 476 us; the launch traced here: 474 us
  waiting for transfers between devices  203 us (43%)
  blocking collectives  97.5 us (20%)
  matrix products  87.3 us (18%)
  other arithmetic  35.1 us (7%)
  local copies, waits for them, and re-layouts  28.1 us (6%)
  between operations  13.9 us (3%)
  starting transfers between devices  8.89 us (2%)
    psum x1, waiting for transfers between devices, local(): summed = lax.psum(query_terms, 'slot')  93.3 us
    psum x1, waiting for transfers between devices, local(): key_total, value_total = lax.psum((key_grad, value_grad), 'conv')  82.7 us
    psum x1, blocking collectives, local(): row_sum = lax.psum(partial_sum, 'slot')  61.4 us
    all_gather x2, blocking collectives, merged(): everything = jax.tree.map(lambda part: lax.all_gather(part, axis), x)  36.1 us
    dot_general x8, matrix products, gradient_products(): jnp.einsum('rkgd,skd->rkgs', grad_block, value_half, preferred_element_ty...  32.8 us
    dot_general x12, matrix products, masked_scores(): jnp.einsum('rkgd,skd->rkgs', query_block, key_half, preferred_element_typ...  30.3 us
    all_to_all x1, waiting for transfers between devices, jax.lax.all_to_all(jnp.stack([page for _ in range(jax.lax.axis_size('slot...  25.4 us
    add x15, other arithmetic, merge_pairs(): earlier[1] * jnp.exp(earlier[0] - largest)  13.6 us
  transfers between devices with their start and end apart: 4, of which 3 were waited for; matrix products, arithmetic and copies ran while one was open for 12% of the time, Pallas kernels for 0%

profile of v1, /device:TPU:1, one launch (start us, length us, event | category | flops | bytes accessed | tf_op | source)
XLA Modules:
  0.0 474.1 jit_solution(197604858819548774)
XLA Ops:
  7.2 2.6 stack.8
  9.8 8.8 %all-to-all-start = ((bf16[16,16,32,128]{3,2,1,0:T(8,128)(2,1)}), bf16[16,16,32,128]{3,2,1,0:T(8,128)(2,1)}, u32[]{:S(2)}, u32[]{:S(2)}) async-start(bf16[16,16,32,128]{3,2,1,0:T(8,128)(2,1)} %stack.8), calls=%async_computation | async-start | bytes 4194304 | tf_op jit(solution)/shard_map/all_to_all | solution.py:14
  19.5 1.8 copy.70
  22.4 25.4 %all-to-all-done = bf16[16,16,32,128]{3,2,1,0:T(8,128)(2,1)} async-done(((bf16[16,16,32,128]{3,2,1,0:T(8,128)(2,1)}), bf16[16,16,32,128]{3,2,1,0:T(8,128)(2,1)}, u32[]{:S(2)}, u32[]{:S(2)}) %all-to-all-start) | async-done | bytes 2097184 | tf_op jit(solution)/shard_map/all_to_all | solution.py:14
  47.8 3.3 copy.50
  51.1 23.2 %while.54 = (s32[]{:T(128)}, f32[4,64,2,16]{1,3,2,0:T(8,128)S(1)}, f32[4,64,2,16]{1,3,2,0:T(8,128)S(1)}, pred[4,64,1024]{2,1,0:T(8,128)(4,1)S(1)}, bf16[4,64,2,1...) while((s32[]{:T(128)}, f32[4,64,2,16]{1,3,2,0:T(8,128)S(1)}, ...), condition=%wide.region_3.4_spmd, body=%wide.region_0.3_spmd.sunk | while | flops 553644032 | bytes 18210912 | solution.py:82
  51.1 2.8 bitcast_reduce_fusion.2
  53.8 2.8 fusion.87
  56.9 2.8 bitcast_reduce_fusion.2
  59.6 2.8 fusion.87
  62.7 2.8 bitcast_reduce_fusion.2
  65.4 2.8 fusion.87
  68.4 2.8 bitcast_reduce_fusion.2
  71.2 2.8 fusion.87
  74.2 17.3 %all-gather.1 = f32[64,64,2,16]{1,3,2,0:T(8,128)S(1)} all-gather(f32[4,64,2,16]{1,3,2,0:T(8,128)S(1)} %get-tuple-element.272), channel_id=3, replica_groups=mesh['slot'=16,'head'=2,'conv'=4] {'slot'}, dimensions={0}, use_global_device_ids=true | all-gather | bytes 557056 | tf_op jit(solution)/shard_map/all_gather | solution.py:25
  91.5 18.8 %all-gather = f32[64,64,2,16]{1,3,2,0:T(8,128)S(1)} all-gather(f32[4,64,2,16]{1,3,2,0:T(8,128)S(1)} %get-tuple-element.271), channel_id=2, replica_groups=mesh['slot'=16,'head'=2,'conv'=4] {'slot'}, dimensions={0}, use_global_device_ids=true | all-gather | bytes 557056 | tf_op jit(solution)/shard_map/all_gather | solution.py:25
  110.4 1.0 copy-done.1
  111.3 13.9 %while.55 = (s32[]{:T(128)}, f32[4,64,2,16]{1,3,2,0:T(8,128)S(1)}, f32[4,64,2,16]{1,3,2,0:T(8,128)S(1)}, f32[16,4,64,2,16]{2,4,3,1,0:T(8,128)}, f32[16,4,64,2,16...) while((s32[]{:T(128)}, f32[4,64,2,16]{1,3,2,0:T(8,128)S(1)}, f32[4,64,2,16]{1,3,2,0:T(8,128)S(1)}, ...), condition=%wide.region_5.6_spmd, body=%wide.region_4.5_spmd.sunk | while | flops 49157 | bytes 196731 | solution.py:31
  112.3 0.9 fusion.88
  123.4 0.9 fusion.88
  125.6 3.3 copy.51
  128.9 31.2 %while.56 = (s32[]{:T(128)}, f32[4,64,2,16]{3,1,2,0:T(8,128)}, pred[4,64,1024]{2,1,0:T(8,128)(4,1)S(1)}, bf16[4,64,2,16,128]{4,3,1,2,0:T(8,128)(2,1)}, bf16[1024...) while((s32[]{:T(128)}, f32[4,64,2,16]{3,1,2,0:T(8,128)}, ...), condition=%wide.region_8.9_spmd, body=%wide.region_6.8_spmd.sunk | while | flops 1086322688 | bytes 21397652 | solution.py:91
  128.9 2.4 fusion.93
  131.4 4.7 %fusion.94 = f32[64,2,16]{2,0,1:T(8,128)S(1)} fusion(f32[2,64,16,1024]{3,2,1,0:T(8,128)S(1)} %fusion.93, f32[64,2,16]{2,0,1:T(8,128)S(1)} %dynamic-slice_bitcast_fusion.12, pred[64,1024]{1,0:T(8,128)(4,1)S(1)} %dynamic-slice_bitcast_fusion.13, bf16[1024,2,128]{2,0,1:T(8,128)(2,1)S(1)} %copy-done.3, ...), kind=kOutput, calls=%fused_computation.20.clone.1 | convolution fusion | flops 549451776 | bytes 9641988 | tf_op jit(solution)/shard_map/while/body/eval_jaxpr/rkgd,skd->rkgs/dot_general | solution.py:72
  136.8 2.4 fusion.93
  139.2 4.7 %fusion.94 = f32[64,2,16]{2,0,1:T(8,128)S(1)} fusion(f32[2,64,16,1024]{3,2,1,0:T(8,128)S(1)} %fusion.93, f32[64,2,16]{2,0,1:T(8,128)S(1)} %dynamic-slice_bitcast_fusion.12, pred[64,1024]{1,0:T(8,128)(4,1)S(1)} %dynamic-slice_bitcast_fusion.13, bf16[1024,2,128]{2,0,1:T(8,128)(2,1)S(1)} %copy-done.3, ...), kind=kOutput, calls=%fused_computation.20.clone.1 | convolution fusion | flops 549451776 | bytes 9641988 | tf_op jit(solution)/shard_map/while/body/eval_jaxpr/rkgd,skd->rkgs/dot_general | solution.py:72
  144.6 2.4 fusion.93
  146.9 4.7 %fusion.94 = f32[64,2,16]{2,0,1:T(8,128)S(1)} fusion(f32[2,64,16,1024]{3,2,1,0:T(8,128)S(1)} %fusion.93, f32[64,2,16]{2,0,1:T(8,128)S(1)} %dynamic-slice_bitcast_fusion.12, pred[64,1024]{1,0:T(8,128)(4,1)S(1)} %dynamic-slice_bitcast_fusion.13, bf16[1024,2,128]{2,0,1:T(8,128)(2,1)S(1)} %copy-done.3, ...), kind=kOutput, calls=%fused_computation.20.clone.1 | convolution fusion | flops 549451776 | bytes 9641988 | tf_op jit(solution)/shard_map/while/body/eval_jaxpr/rkgd,skd->rkgs/dot_general | solution.py:72
  152.4 2.4 fusion.93
  154.7 4.7 %fusion.94 = f32[64,2,16]{2,0,1:T(8,128)S(1)} fusion(f32[2,64,16,1024]{3,2,1,0:T(8,128)S(1)} %fusion.93, f32[64,2,16]{2,0,1:T(8,128)S(1)} %dynamic-slice_bitcast_fusion.12, pred[64,1024]{1,0:T(8,128)(4,1)S(1)} %dynamic-slice_bitcast_fusion.13, bf16[1024,2,128]{2,0,1:T(8,128)(2,1)S(1)} %copy-done.3, ...), kind=kOutput, calls=%fused_computation.20.clone.1 | convolution fusion | flops 549451776 | bytes 9641988 | tf_op jit(solution)/shard_map/while/body/eval_jaxpr/rkgd,skd->rkgs/dot_general | solution.py:72
  160.1 61.4 %psum.28 = f32[4,64,2,16]{3,1,2,0:T(8,128)S(1)} all-reduce(f32[4,64,2,16]{3,1,2,0:T(8,128)} %get-tuple-element.275), channel_id=1, replica_groups=mesh['slot'=16,'head'=2,'conv'=4] {'slot'}, use_global_device_ids=true, to_apply=%region_9.10 | all-reduce | flops 8192 | bytes 65536 | tf_op jit(solution)/shard_map/psum | solution.py:92
  221.5 52.7 %while.57 = (s32[]{:T(128)}, f32[1024,2,128]{0,2,1:T(8,128)S(1)}, f32[1024,2,128]{0,2,1:T(8,128)S(1)}, f32[4,64,2,16,128]{4,3,2,1,0:T(8,128)}, bf16[4,64,2,16,12...) while((s32[]{:T(128)}, f32[1024,2,128]{0,2,1:T(8,128)S(1)}, ...), condition=%wide.region_11.12_spmd.clone, body=%wide.region_10.11_spmd.clone.sunk | while | flops 2711093248 | bytes 59867360 | solution.py:118
  221.6 2.4 fusion.105
  224.0 2.7 fusion.108
  226.7 3.5 fusion.106
  230.2 2.1 fusion.107
  232.3 1.2 fusion.109
  233.6 1.1 copy_dynamic-update-slice_fusion.2
  234.7 2.4 fusion.105
  237.2 2.7 fusion.108
  239.9 3.5 fusion.106
  243.4 2.1 fusion.107
  245.5 1.2 fusion.109
  246.7 1.2 copy_dynamic-update-slice_fusion.2
  247.9 2.4 fusion.105
  250.4 2.7 fusion.108
  253.1 3.5 fusion.106
  256.6 2.1 fusion.107
  258.7 1.2 fusion.109
  259.9 1.1 copy_dynamic-update-slice_fusion.2
  261.1 2.4 fusion.105
  263.6 2.7 fusion.108
  266.3 3.5 fusion.106
  269.7 2.1 fusion.107
  271.8 1.2 fusion.109
  273.1 1.2 copy_dynamic-update-slice_fusion.2
  274.2 1.3 copy.52
  275.5 1.3 copy.53
  277.6 82.7 %all-reduce.6.cloned.1.call-done = (f32[1,1024,2,128]{3,2,1,0:T(2,128)}, f32[1,1024,2,128]{3,2,1,0:T(2,128)}) async-done(((f32[1,1024,2,128]{3,2,1,0:T(2,128)}, f32[1,1024,2,128]{3,2,1,0:T(2,128)}), (f32[1,1024,2,128]{3,2,1,0:T(2,128)}, f32[1,1024,2,128]{3,2,1,0:T(2,128)})) %all-reduce.6.cloned.1.call-update) | async-done | bytes 2097168 | tf_op jit(solution)/shard_map/psum | solution.py:127
  360.2 1.3 constant_dynamic-update-slice_fusion.3
  361.5 1.4 constant_dynamic-update-slice_fusion.2
  362.9 9.8 %divide_subtract_fusion = (f32[2,1024,2,128]{3,2,1,0:T(2,128)}, f32[2,1024,2,128]{3,2,1,0:T(2,128)}, f32[2,1024,2,128]{3,2,1,0:T(2,128)}) fusion(f32[2,1024,2,128]{3,2,1,0:T(2,128)} %param.19, f32[2,1024,2,128]{3,2,1,0:T(2,128)S(1)} %constant_dynamic-update-slice_fusion.2, f32[2,1024,2,128]{3,2,1,0:T(2,128)} %param.20, f32[2,1024,2,128]{3,2,1,0:T(2,128)} %param.21), kind=kLoop, calls=%fused_computation.80 | loop fusion | flops 6291456 | bytes 14680064 | tf_op jit(solution)/shard_map/sub | solution.py:133
  372.7 93.3 %all-reduce.4.cloned.1.call-done = f32[256,32,128]{2,1,0:T(8,128)} async-done(((f32[256,32,128]{2,1,0:T(8,128)}), f32[256,32,128]{2,1,0:T(8,128)}) %all-reduce.4.cloned.1.call-update) | async-done | bytes 4194320 | tf_op jit(solution)/shard_map/psum | solution.py:124
  465.9 1.7 constant_dynamic-slice_fusion
  (101 shorter events, 18.2 us)
Async XLA Ops:
  7.2 12.3 %copy-start.6 = (s32[256]{0:T(256)S(1)}, s32[256]{0:T(256)}, u32[]{:S(2)}) copy-start(s32[256]{0:T(256)} %param.17) | copy-start | bytes 3076
  9.8 11.5 %copy-start.5 = (s32[1024]{0:T(1024)S(1)}, s32[1024]{0:T(1024)}, u32[]{:S(2)}) copy-start(s32[1024]{0:T(1024)} %param.18) | copy-start | bytes 12292
  9.8 38.0 %all-to-all-start = ((bf16[16,16,32,128]{3,2,1,0:T(8,128)(2,1)}), bf16[16,16,32,128]{3,2,1,0:T(8,128)(2,1)}, u32[]{:S(2)}, u32[]{:S(2)}) async-start(bf16[16,16,32,128]{3,2,1,0:T(8,128)(2,1)} %stack.8), calls=%async_computation | async-start | bytes 4194304 | tf_op jit(solution)/shard_map/all_to_all | solution.py:14
  18.6 107.0 %all-gather.4.cloned.1.call-start = ((), (), s32[]{:S(2)}) async-start(), calls=%async_computation.1 | async-start | bytes 2228224 | tf_op jit(solution)/shard_map/all_gather | solution.py:45
  19.3 340.9 %all-reduce.6.cloned.1.call-start = ((), (), s32[]{:S(2)}) async-start(), calls=%async_computation.3 | async-start | bytes 4194304 | tf_op jit(solution)/shard_map/psum | solution.py:127
  110.4 1.0 copy-start.1
  128.9 92.6 %copy-start.2 = (f32[1024,2,128]{0,2,1:T(8,128)S(1)}, f32[1024,2,128]{0,2,1:T(8,128)}, u32[]{:S(2)}) copy-start(f32[1024,2,128]{0,2,1:T(8,128)} %custom-call.1) | copy-start | bytes 3145732
  128.9 2.4 copy-start.3
  136.8 2.4 copy-start.3
  144.6 2.4 copy-start.3
  152.3 2.4 copy-start.3
  221.6 2.5 copy-start
  224.0 2.7 copy-start.4
  234.7 2.5 copy-start
  237.2 2.7 copy-start.4
  247.9 2.5 copy-start
  250.4 2.7 copy-start.4
  261.1 2.5 copy-start
  263.6 2.7 copy-start.4
  276.8 189.1 %all-reduce.4.cloned.1.call-start = ((), (), s32[]{:S(2)}) async-start(), calls=%async_computation.2 | async-start | bytes 8388608 | tf_op jit(solution)/shard_map/psum | solution.py:124
Sparse Core Ops, SparseCore 0:
  21.5 52.4 all-gather.3
  277.0 83.2 all-reduce.5
  363.6 102.2 all-reduce.3
